TPU v7x, 32 devices: a whole 2x2x4 slice. The times are simulated.
32 devices in a mesh: wide: 4 (over x, core), sixteen: 8 (over z, y).
Axes of the slice: x: 2, y: 2, z: 4, core: 2. Of those that a mesh axis runs over, the one named last changes fastest.
Arguments:
- features: float32 [4, 8, 512, 128], P('wide', 'sixteen'), may hold values from -6 to 6
- positions: float32 [4, 8, 3, 512], P('wide', 'sixteen'), may hold values from 0 to 1, as said below
- tile_lists: int32 [4, 8, 4, 16], P('wide', 'sixteen'), may hold values from 0 to 36, as said below
- value_proj: float32 [128, 128], replicated, may hold values from -0.5 to 0.5
- radial_mix: float32 [16, 128], replicated, may hold values from -1.5 to 1.5
- charge_proj: float32 [128, 128], replicated, may hold values from -0.5 to 0.5
- screening: float32 [128], P(('wide', 'sixteen')), may hold values from 20 to 200
- smearing: float32 [128], P(('wide', 'sixteen')), may hold values from 0.003 to 0.02
- mesh_gain: float32 [128], replicated, may hold values from 0.25 to 1.75
- mesh_up: float32 [128, 256], replicated, may hold values from -0.5 to 0.5
- mesh_down: float32 [256, 128], replicated, may hold values from -0.375 to 0.375
- long_proj: float32 [128, 128], replicated, may hold values from -0.5 to 0.5
- atom_gain: float32 [128], replicated, may hold values from 0.25 to 1.75
- atom_up: float32 [128, 256], replicated, may hold values from -0.5 to 0.5
- atom_down: float32 [256, 128], replicated, may hold values from -0.375 to 0.375
Outputs:
- updated: float32 [4, 8, 512, 128], P('wide', 'sixteen')
Inputs may be any that keep to these rules, and one draw needn't show every extreme that they name: `tile_lists`: each list of tile t of a block holds codes nb * 4 + t2 of tiles of the 3 x 3 blocks around it with (t2 - t) mod 4 equal to 0, 1 or 3; its first entry is the tile itself, 16 + t; its live entries are distinct; empty entries hold 36 and stand after all live ones; every list has 1 to 16 live entries and some list has 16. `positions`: the third coordinate of atom a of a block lies between a / 512 and (a + 1) / 512.
All inputs are finite; a program needn't handle non-finite values.
Results may differ from a plain program's by a relative error of at most 0.0003.
Values sent between devices are 32-bit elements; how exact they have to be, the bound alone decides.
A program may use at most 128 MiB of HBM per device.

v0:
```python
import jax
import jax.numpy as jnp
from jax import lax
from jax.sharding import PartitionSpec as P

MESH = 64
TILE = 128


exact = lax.Precision.HIGHEST


def extended_2(block, sides, width):
    for axis, dim in sides:
        count = lax.axis_size(axis)
        forward = [(i, i + 1) for i in range(count - 1)]
        forward.append((count - 1, 0))
        backward = [(target, source) for source, target in forward]
        low = lax.ppermute(
            lax.slice_in_dim(block, block.shape[dim] - width, None, axis=dim), axis, forward
        )
        high = lax.ppermute(lax.slice_in_dim(block, 0, width, axis=dim), axis, backward)
        block = jnp.concatenate([low, block, high], axis=dim)
    return block


def passed_along(array, axis, by):
    count = lax.axis_size(axis)
    return lax.ppermute(array, axis, [(i, (i + by) % count) for i in range(count)])


def short_range(near_values, near_positions, tile_codes, radial_mix, wide_count, sixteen_count):
    atom_count = near_values.shape[2]
    feature_width = near_values.shape[3]
    tiles_per = atom_count // TILE
    basis_count = radial_mix.shape[0]
    empty_code = 9 * tiles_per
    cutoff = 0.8 / max(wide_count, sixteen_count)
    sharpness = 0.5 * (basis_count - 1) ** 2
    centres = jnp.arange(basis_count).astype(jnp.float32) / (basis_count - 1)
    offsets = jnp.arange(3).astype(jnp.float32) - 1.0
    global_x = (near_positions[:, :, 0, :] + offsets[:, None, None]) / wide_count
    global_y = (near_positions[:, :, 1, :] + offsets[None, :, None]) / sixteen_count
    global_z = near_positions[:, :, 2, :]
    placed = jnp.stack([global_x, global_y, global_z], axis=2)
    source_pos = (
        placed.reshape(9, 3, tiles_per, TILE).transpose(0, 2, 1, 3).reshape(empty_code, 3, TILE)
    )
    source_val = near_values.reshape(empty_code, TILE, feature_width)
    own_pos = source_pos[4 * tiles_per : 5 * tiles_per]
    own_codes = 4 * tiles_per + jnp.arange(tiles_per, dtype=jnp.int32)
    diagonal = jnp.eye(TILE, dtype=bool)

    def one_slot(slot_index, running):
        slot_codes = tile_codes[:, slot_index]
        is_live = slot_codes < empty_code
        chosen = jnp.minimum(slot_codes, empty_code - 1)
        other_pos = source_pos[chosen]
        other_val = source_val[chosen]
        offset_vec = other_pos[:, :, None, :] - own_pos[:, :, :, None]
        delta_z = offset_vec[:, 2] - jnp.floor(offset_vec[:, 2] + 0.5)
        radius = jnp.sqrt(offset_vec[:, 0] ** 2 + offset_vec[:, 1] ** 2 + delta_z**2) / cutoff
        envelope = jnp.where(radius < 1.0, 0.5 * (jnp.cos(jnp.pi * radius) + 1.0), 0.0)
        itself = (slot_codes == own_codes)[:, None, None] & diagonal[None]
        envelope = jnp.where(is_live[:, None, None] & ~itself, envelope, 0.0)
        basis_vals = (
            jnp.exp(-sharpness * (radius[:, None] - centres[None, :, None, None]) ** 2)
            * envelope[:, None]
        )
        partial_sum = jnp.einsum("tbij,tjc->tbic", basis_vals, other_val, precision=exact)
        return running + jnp.einsum("tbic,bc->tic", partial_sum, radial_mix, precision=exact)

    live_slots = tile_codes.shape[1]
    running = lax.fori_loop(
        0, live_slots, one_slot, jnp.zeros((tiles_per, TILE, feature_width), jnp.float32)
    )
    return running.reshape(atom_count, feature_width)


def slab_stencil(own_pos, slab_x, slab_y):
    limits = jnp.array([slab_x - 1, slab_y - 1, MESH - 1], jnp.int32)
    coords = jnp.stack([own_pos[0] * slab_x, own_pos[1] * slab_y, own_pos[2] * MESH])
    base_cell = jnp.minimum(jnp.floor(coords).astype(jnp.int32), limits[:, None])
    fraction = coords - base_cell.astype(jnp.float32)
    cell_list = []
    weights = []
    for corner in range(8):
        corner_steps = (corner // 4, corner // 2 % 2, corner % 2)
        index_x = base_cell[0] + corner_steps[0]
        index_y = base_cell[1] + corner_steps[1]
        index_z = (base_cell[2] + corner_steps[2]) % MESH
        cell_list.append((index_x * (slab_y + 1) + index_y) * MESH + index_z)
        weight = jnp.ones(coords.shape[1], jnp.float32)
        for dimension in range(3):
            if corner_steps[dimension]:
                weight = weight * fraction[dimension]
            else:
                weight = weight * (1.0 - fraction[dimension])
        weights.append(weight)
    return (cell_list, weights)


def filter_kernel(screening, smearing):
    sample_index = jnp.arange(MESH, dtype=jnp.int32)
    signed = jnp.where(sample_index < MESH // 2, sample_index, sample_index - MESH).astype(
        jnp.float32
    )
    wavenumber = 2.0 * jnp.pi * signed
    squares = (
        wavenumber[:, None, None] ** 2
        + wavenumber[None, :, None] ** 2
        + wavenumber[None, None, :] ** 2
    )
    kappa_sq = screening[:, None, None, None] ** 2
    return (
        kappa_sq
        * jnp.exp(-0.5 * squares[None] * smearing[:, None, None, None] ** 2)
        / (squares[None] + kappa_sq)
    )


def dft_tables(length):
    sample_index = jnp.arange(length, dtype=jnp.int32)
    phase_index = sample_index[:, None] * sample_index[None, :] % length
    angle_grid = phase_index.astype(jnp.float32) * (2.0 * jnp.pi / length)
    return (jnp.cos(angle_grid), jnp.sin(angle_grid))


def rotate(real_part, imag_part, table_cos, table_sin, subscripts, direction):
    cos_real = jnp.einsum(subscripts, real_part, table_cos, precision=exact)
    sin_real = jnp.einsum(subscripts, real_part, table_sin, precision=exact)
    cos_imag = jnp.einsum(subscripts, imag_part, table_cos, precision=exact)
    sin_imag = jnp.einsum(subscripts, imag_part, table_sin, precision=exact)
    return (cos_real - direction * sin_imag, cos_imag + direction * sin_real)


def smooth_field(field_grid, screening, smearing):
    table_cos, table_sin = dft_tables(MESH)
    real_part = jnp.einsum("cxyz,zk->cxyk", field_grid, table_cos, precision=exact)
    imag_part = -jnp.einsum("cxyz,zk->cxyk", field_grid, table_sin, precision=exact)
    real_part, imag_part = rotate(real_part, imag_part, table_cos, table_sin, "cxyz,yk->cxkz", -1.0)
    real_part, imag_part = rotate(real_part, imag_part, table_cos, table_sin, "cxyz,xk->ckyz", -1.0)
    kernel = filter_kernel(screening, smearing)
    real_part = real_part * kernel
    imag_part = imag_part * kernel
    real_part, imag_part = rotate(real_part, imag_part, table_cos, table_sin, "cxyz,xk->ckyz", 1.0)
    real_part, imag_part = rotate(real_part, imag_part, table_cos, table_sin, "cxyz,yk->cxkz", 1.0)
    result_grid = jnp.einsum("cxyz,zk->cxyk", real_part, table_cos, precision=exact) - jnp.einsum(
        "cxyz,zk->cxyk", imag_part, table_sin, precision=exact
    )
    return result_grid / MESH**3


def mesh_rows(by_cells, mesh_gain, mesh_up, mesh_down):
    inverse_rms = lax.rsqrt(jnp.mean(by_cells**2, axis=1, keepdims=True) + 1e-06)
    normed = by_cells * inverse_rms * mesh_gain[None, :]
    hidden = jax.nn.silu(jnp.dot(normed, mesh_up, precision=exact))
    return jnp.dot(hidden, mesh_down, precision=exact)


def on_device(
    features,
    positions,
    tile_lists,
    value_proj,
    radial_mix,
    charge_proj,
    screening,
    smearing,
    mesh_gain,
    mesh_up,
    mesh_down,
    long_proj,
    atom_gain,
    atom_up,
    atom_down,
):
    wide_count = lax.axis_size("wide")
    sixteen_count = lax.axis_size("sixteen")
    devices = wide_count * sixteen_count
    channels = charge_proj.shape[1]
    local_channels = screening.shape[0]
    slab_x = MESH // wide_count
    slab_y = MESH // sixteen_count
    slab_cells = slab_x * slab_y * MESH
    values = jnp.einsum("xyaf,fg->xyag", features, value_proj, precision=exact)
    near_values, near_positions = (
        extended_2(values, (("wide", 0), ("sixteen", 1)), 1),
        extended_2(positions, (("wide", 0), ("sixteen", 1)), 1),
    )
    own_features = features[0, 0]
    own_pos = positions[0, 0]
    charges = jnp.dot(own_features, charge_proj, precision=exact)
    cell_list, weights = slab_stencil(own_pos, slab_x, slab_y)
    spread = jnp.zeros(((slab_x + 1) * (slab_y + 1) * MESH, channels), jnp.float32)
    for corner in range(8):
        spread = spread.at[cell_list[corner]].add(weights[corner][:, None] * charges)
    spread = spread.reshape(slab_x + 1, slab_y + 1, MESH, channels)
    from_below = passed_along(spread[slab_x], "wide", 1)
    spread = spread[:slab_x].at[0].add(from_below)
    from_left = passed_along(spread[:, slab_y], "sixteen", 1)
    slab = spread[:, :slab_y].at[:, 0].add(from_left)
    messages = short_range(
        near_values, near_positions, tile_lists[0, 0], radial_mix, wide_count, sixteen_count
    )
    grouped = lax.all_to_all(
        slab.reshape(slab_cells, devices, local_channels),
        ("wide", "sixteen"),
        split_axis=1,
        concat_axis=1,
        tiled=True,
    )
    grouped = grouped.reshape(slab_x, slab_y, MESH, wide_count, sixteen_count, local_channels)
    field_grid = grouped.transpose(5, 3, 0, 4, 1, 2).reshape(local_channels, MESH, MESH, MESH)
    potential = smooth_field(field_grid, screening, smearing)
    outgoing = potential.reshape(
        local_channels, wide_count, slab_x, sixteen_count, slab_y, MESH
    ).transpose(2, 4, 5, 1, 3, 0)
    returned = lax.all_to_all(
        outgoing.reshape(slab_cells, devices, local_channels),
        ("wide", "sixteen"),
        split_axis=1,
        concat_axis=1,
        tiled=True,
    )
    by_cells = returned.reshape(slab_cells, channels)
    mesh_out = mesh_rows(by_cells, mesh_gain, mesh_up, mesh_down).reshape(
        slab_x, slab_y, MESH, channels
    )
    from_above = passed_along(mesh_out[0], "wide", -1)
    extended = jnp.concatenate([mesh_out, from_above[None]], axis=0)
    from_right = passed_along(extended[:, 0], "sixteen", -1)
    extended = jnp.concatenate([extended, from_right[:, None]], axis=1).reshape(-1, channels)
    at_atoms = jnp.zeros((own_features.shape[0], channels), jnp.float32)
    for corner in range(8):
        at_atoms = at_atoms + weights[corner][:, None] * extended[cell_list[corner]]
    long_terms = jnp.dot(at_atoms, long_proj, precision=exact)
    summed = own_features + messages + long_terms
    inverse_rms = lax.rsqrt(jnp.mean(summed**2, axis=-1, keepdims=True) + 1e-06)
    normed = summed * inverse_rms * atom_gain
    hidden = jax.nn.silu(jnp.dot(normed, atom_up, precision=exact))
    updated = summed + jnp.dot(hidden, atom_down, precision=exact)
    return updated[None, None]


def solution(mesh):
    in_specs = (
        P("wide", "sixteen", None, None),
        P("wide", "sixteen", None, None),
        P("wide", "sixteen", None, None),
        P(),
        P(),
        P(),
        P(("wide", "sixteen")),
        P(("wide", "sixteen")),
        P(),
        P(),
        P(),
        P(),
        P(),
        P(),
        P(),
    )
    out_specs = P("wide", "sixteen", None, None)
    return jax.shard_map(
        on_device, mesh=mesh, in_specs=in_specs, out_specs=out_specs, check_vma=False
    )
```

profile of v0, /device:TPU:0, one launch (start us, length us, event | category | flops | bytes accessed | tf_op | source)
XLA Modules:
  0.0 866.0 jit_solution(4879949012899831171)
XLA Ops:
  76.5 11.9 %collective-permute-done.9 = f32[16,64,128]{2,1,0:T(8,128)S(1)} collective-permute-done((f32[16,64,128]{2,1,0:T(8,128)S(1)}, f32[16,64,128]{2,1,0:T(8,128)S(1)}, u32[]{:S(2)}, u32[]{:S(2)}) %collective-permute-start.9) | collective-permute-done | bytes 524320 | tf_op jit(solution)/shard_map/ppermute | solution.py:29
  113.3 93.4 %all-to-all-done = f32[8192,32,4]{0,2,1:T(4,128)} async-done(((f32[8192,32,4]{0,2,1:T(4,128)}), f32[8192,32,4]{0,2,1:T(4,128)}, u32[]{:S(2)}, u32[]{:S(2)}) %all-to-all-start) | async-done | bytes 4194336 | tf_op jit(solution)/shard_map/all_to_all | solution.py:206
  241.4 10.0 %fusion.147 = f32[64,4,64,64]{3,0,2,1:T(8,128)} fusion(f32[4,64,64,64]{3,2,1,0:T(8,128)S(1)} %fusion.155), kind=kOutput, calls=%fused_computation.193 | convolution fusion | flops 805363712 | bytes 8388608 | tf_op jit(solution)/shard_map/cxyz,yk->cxkz/dot_general | solution.py:131
  251.3 9.6 %fusion.162 = f32[64,4,64,64]{3,0,2,1:T(8,128)} fusion(f32[4,64,64,64]{3,2,1,0:T(8,128)S(1)} %fusion.155), kind=kOutput, calls=%fused_computation.208 | convolution fusion | flops 805363712 | bytes 8388608 | tf_op jit(solution)/shard_map/cxyz,yk->cxkz/dot_general | solution.py:130
  261.0 11.3 %add_bitcast_fusion.1 = f32[4,64,64,64]{3,2,1,0:T(8,128)S(1)} fusion(f32[64,4,64,64]{3,0,2,1:T(8,128)} %fusion.147, f32[4,64,64,64]{3,2,1,0:T(8,128)S(1)} %fusion.151), kind=kOutput, calls=%fused_computation.70 | convolution fusion | flops 808509440 | bytes 12582912 | tf_op jit(solution)/shard_map/cxyz,yk->cxkz/dot_general | solution.py:132
  272.3 13.3 %fusion.44 = f32[64,4,64,64]{3,0,2,1:T(8,128)} fusion(f32[4,64,64,64]{3,2,1,0:T(8,128)S(1)} %add_bitcast_fusion.1), kind=kOutput, calls=%fused_computation.80 | convolution fusion | flops 805363712 | bytes 8388608 | tf_op jit(solution)/shard_map/cxyz,xk->ckyz/dot_general | solution.py:132
  285.6 13.6 %fusion.46 = f32[64,4,64,64]{3,0,2,1:T(8,128)} fusion(f32[4,64,64,64]{3,2,1,0:T(8,128)S(1)} %add_bitcast_fusion.1), kind=kOutput, calls=%fused_computation.82 | convolution fusion | flops 805363712 | bytes 8388608 | tf_op jit(solution)/shard_map/cxyz,xk->ckyz/dot_general | solution.py:133
  310.6 20.6 %bitcast_multiply_fusion = f32[4,64,64,64]{3,1,2,0:T(8,128)S(1)} fusion(f32[64,4,64,64]{3,0,2,1:T(8,128)} %fusion.44, f32[64,64,64]{2,0,1:T(8,128)} %get-tuple-element.372, f32[4]{0:T(128)S(1)} %integer_pow.94, f32[64,64,64]{2,0,1:T(8,128)} %get-tuple-element.371, f32[4]{0:T(128)S(1)} %integer_pow.92, f32[4,64,64,64]{3,2,1,0:T(8,128)S(1)} %subtract_bitcast_fusion.1), kind=kOutput, calls=%fused_computation.55 | convolution fusion | flops 812703744 | bytes 14680096 | tf_op jit(solution)/shard_map/cxyz,xk->ckyz/dot_general | solution.py:131
  331.2 20.3 %bitcast_multiply_fusion.1 = f32[4,64,64,64]{3,1,2,0:T(8,128)S(1)} fusion(f32[64,4,64,64]{3,0,2,1:T(8,128)} %fusion.46, f32[64,64,64]{2,0,1:T(8,128)} %get-tuple-element.372, f32[4]{0:T(128)S(1)} %integer_pow.94, f32[64,64,64]{2,0,1:T(8,128)} %get-tuple-element.371, f32[4]{0:T(128)S(1)} %integer_pow.92, f32[4,64,64,64]{3,2,1,0:T(8,128)} %copy-done.2), kind=kOutput, calls=%fused_computation.56 | convolution fusion | flops 812703744 | bytes 14680096 | tf_op jit(solution)/shard_map/cxyz,xk->ckyz/dot_general | solution.py:130
  351.5 9.7 %fusion.165 = f32[64,4,64,64]{3,0,2,1:T(8,128)} fusion(f32[4,64,64,64]{3,1,2,0:T(8,128)S(1)} %bitcast_multiply_fusion.1), kind=kOutput, calls=%fused_computation.211 | convolution fusion | flops 805363712 | bytes 8388608 | tf_op jit(solution)/shard_map/cxyz,xk->ckyz/dot_general | solution.py:130
  361.2 9.8 %fusion.158 = f32[64,4,64,64]{3,0,2,1:T(8,128)} fusion(f32[4,64,64,64]{3,1,2,0:T(8,128)S(1)} %bitcast_multiply_fusion), kind=kOutput, calls=%fused_computation.204 | convolution fusion | flops 805363712 | bytes 8388608 | tf_op jit(solution)/shard_map/cxyz,xk->ckyz/dot_general | solution.py:132
  371.0 10.1 %add_bitcast_fusion = f32[4,64,64,64]{3,1,2,0:T(8,128)S(1)} fusion(f32[64,4,64,64]{3,0,2,1:T(8,128)} %fusion.158, f32[4,64,64,64]{3,1,2,0:T(8,128)S(1)} %bitcast_multiply_fusion.1), kind=kOutput, calls=%fused_computation.67 | convolution fusion | flops 806412288 | bytes 12582912 | tf_op jit(solution)/shard_map/cxyz,xk->ckyz/dot_general | solution.py:131
  381.1 12.0 %fusion.36 = f32[64,4,64,64]{3,0,2,1:T(8,128)S(1)} fusion(f32[4,64,64,64]{3,1,2,0:T(8,128)S(1)} %add_bitcast_fusion), kind=kOutput, calls=%fused_computation.72 | convolution fusion | flops 805363712 | bytes 8388608 | tf_op jit(solution)/shard_map/cxyz,yk->cxkz/dot_general | solution.py:132
  393.2 13.6 %fusion.38 = f32[64,4,64,64]{3,0,2,1:T(8,128)} fusion(f32[4,64,64,64]{3,1,2,0:T(8,128)S(1)} %add_bitcast_fusion), kind=kOutput, calls=%fused_computation.74 | convolution fusion | flops 805363712 | bytes 8388608 | tf_op jit(solution)/shard_map/cxyz,yk->cxkz/dot_general | solution.py:133
  406.7 10.1 %subtract_bitcast_fusion = f32[4,64,64,64]{3,1,2,0:T(8,128)S(1)} fusion(f32[64,4,64,64]{3,0,2,1:T(8,128)} %fusion.165, f32[4,64,64,64]{3,1,2,0:T(8,128)S(1)} %bitcast_multiply_fusion), kind=kOutput, calls=%fused_computation.68 | convolution fusion | flops 806412288 | bytes 12582912 | tf_op jit(solution)/shard_map/cxyz,xk->ckyz/dot_general | solution.py:133
  416.8 12.0 %fusion.40 = f32[64,4,64,64]{3,0,2,1:T(8,128)S(1)} fusion(f32[4,64,64,64]{3,1,2,0:T(8,128)S(1)} %subtract_bitcast_fusion), kind=kOutput, calls=%fused_computation.76 | convolution fusion | flops 805363712 | bytes 8388608 | tf_op jit(solution)/shard_map/cxyz,yk->cxkz/dot_general | solution.py:131
  428.9 13.5 %fusion.42 = f32[64,4,64,64]{3,0,2,1:T(8,128)} fusion(f32[4,64,64,64]{3,1,2,0:T(8,128)S(1)} %subtract_bitcast_fusion), kind=kOutput, calls=%fused_computation.78 | convolution fusion | flops 805363712 | bytes 8388608 | tf_op jit(solution)/shard_map/cxyz,yk->cxkz/dot_general | solution.py:130
  442.3 9.2 %fusion.24 = f32[4,64,64,64]{3,2,1,0:T(8,128)} fusion(f32[64,4,64,64]{3,0,2,1:T(8,128)S(1)} %fusion.36, f32[64,4,64,64]{3,0,2,1:T(8,128)S(1)} %fusion.40), kind=kOutput, calls=%fused_computation.51 | convolution fusion | flops 806412288 | bytes 12582912 | tf_op jit(solution)/shard_map/cxyz,zk->cxyk/dot_general | solution.py:148
  451.6 12.8 %subtract_multiply_fusion = f32[4,64,64,64]{3,2,1,0:T(8,128)S(1)} fusion(f32[4,64,64,64]{3,2,1,0:T(8,128)} %fusion.24, f32[64,4,64,64]{3,0,2,1:T(8,128)} %fusion.42, f32[64,4,64,64]{3,0,2,1:T(8,128)} %fusion.38), kind=kOutput, calls=%fused_computation.64 | convolution fusion | flops 808509440 | bytes 16777216 | tf_op jit(solution)/shard_map/cxyz,zk->cxyk/dot_general | solution.py:148
  493.4 17.2 %collective-permute-done = f32[1,1,3,512]{3,1,2,0:T(1,128)S(1)} collective-permute-done((f32[1,1,3,512]{3,1,2,0:T(1,128)S(1)}, f32[1,1,3,512]{3,1,2,0:T(1,128)S(1)}, u32[]{:S(2)}, u32[]{:S(2)}) %collective-permute-start) | collective-permute-done | bytes 6176 | tf_op jit(solution)/shard_map/ppermute | solution.py:19
  510.7 13.6 %collective-permute-start.3 = (f32[3,1,3,512]{3,1,2,0:T(1,128)S(1)}, f32[3,1,3,512]{3,1,2,0:T(1,128)S(1)}, u32[]{:S(2)}, u32[]{:S(2)}) collective-permute-start(f32[3,1,3,512]{3,1,2,0:T(1,128)S(1)} %constant_dynamic-update-slice_fusion), channel_id=1, source_target_pairs={{1,0},{2,1},{3,2},{4,3},{5,4},{6,5},{7,6},{0,7},{9,8},{10,9},{11,1... | collective-permute-start | bytes 55304 | tf_op jit(solution)/shard_map/ppermute | solution.py:22
  524.6 34.3 %collective-permute-done.3 = f32[3,1,3,512]{3,1,2,0:T(1,128)S(1)} collective-permute-done((f32[3,1,3,512]{3,1,2,0:T(1,128)S(1)}, f32[3,1,3,512]{3,1,2,0:T(1,128)S(1)}, u32[]{:S(2)}, u32[]{:S(2)}) %collective-permute-start.3) | collective-permute-done | bytes 18464 | tf_op jit(solution)/shard_map/ppermute | solution.py:22
  564.9 35.8 %all-to-all-done.1 = f32[8192,32,4]{0,2,1:T(4,128)} async-done(((f32[8192,32,4]{0,2,1:T(4,128)}), f32[8192,32,4]{0,2,1:T(4,128)}, u32[]{:S(2)}, u32[]{:S(2)}) %all-to-all-start.1) | async-done | bytes 4194336 | tf_op jit(solution)/shard_map/all_to_all | solution.py:219
  631.6 196.4 %while.18 = (s32[]{:T(128)}, f32[4,128,128]{2,1,0:T(8,128)S(1)}, s32[4,16]{0,1:T(8,128)S(1)}, f32[36,3,128]{2,1,0:T(4,128)}, f32[4,3,128]{2,0,1:T(4,128)}, /*ind...) while((s32[]{:T(128)}, f32[4,128,128]{2,1,0:T(8,128)S(1)}, ...), condition=%wide.region_1.2_spmd.clone, body=%wide.region_0.1_spmd.clone.sunk | while | flops 1618363392 | bytes 4557243 | solution.py:74
  (514 shorter events, 445.2 us)
Async XLA Ops:
  0.0 609.1 %copy-start = (f32[128,256]{1,0:T(8,128)S(1)}, f32[128,256]{1,0:T(8,128)}, u32[]{:S(2)}) copy-start(f32[128,256]{1,0:T(8,128)} %param.31) | copy-start | bytes 393220
  2.2 53.7 %copy-start.44 = (s32[512,1]{0,1:T(1,128)}, s32[512,1]{0,1:T(1,128)S(1)}, u32[]{:S(2)}) copy-start(s32[512,1]{0,1:T(1,128)S(1)} %get-tuple-element.351) | copy-start | bytes 6148
  2.3 37.9 %copy-start.50 = (s32[512,1]{0,1:T(1,128)}, s32[512,1]{0,1:T(1,128)S(1)}, u32[]{:S(2)}) copy-start(s32[512,1]{0,1:T(1,128)S(1)} %get-tuple-element.356) | copy-start | bytes 6148
  2.3 45.8 %copy-start.46 = (s32[512,1]{0,1:T(1,128)}, s32[512,1]{0,1:T(1,128)S(1)}, u32[]{:S(2)}) copy-start(s32[512,1]{0,1:T(1,128)S(1)} %get-tuple-element.377) | copy-start | bytes 6148
  3.7 44.4 %copy-start.20 = (f32[512]{0:T(512)}, f32[512]{0:T(512)S(1)}, u32[]{:S(2)}) copy-start(f32[512]{0:T(512)S(1)} %get-tuple-element.385) | copy-start | bytes 6148
  3.7 52.2 %copy-start.14 = (f32[512]{0:T(512)}, f32[512]{0:T(512)S(1)}, u32[]{:S(2)}) copy-start(f32[512]{0:T(512)S(1)} %get-tuple-element.382) | copy-start | bytes 6148
  64.8 6.9 collective-permute-start.8
  71.8 16.6 %collective-permute-start.9 = (f32[16,64,128]{2,1,0:T(8,128)S(1)}, f32[16,64,128]{2,1,0:T(8,128)S(1)}, u32[]{:S(2)}, u32[]{:S(2)}) collective-permute-start(f32[16,64,128]{2,1,0:T(8,128)S(1)} %slice_bitcast_fusion), channel_id=1, source_target_pairs={{0,1},{1,2},{2,3},{3,4},{4,5},{5,6},{6,7},{7,0},{8,9},{9,10},{10,1... | collective-permute-start | bytes 1572872 | tf_op jit(solution)/shard_map/ppermute | solution.py:29
  107.1 99.6 %all-to-all-start = ((f32[8192,32,4]{0,2,1:T(4,128)}), f32[8192,32,4]{0,2,1:T(4,128)}, u32[]{:S(2)}, u32[]{:S(2)}) async-start(f32[8192,32,4]{0,2,1:T(4,128)} %reshape.763), calls=%async_computation | async-start | bytes 8388608 | tf_op jit(solution)/shard_map/all_to_all | solution.py:206
  476.9 47.6 %copy-start.55 = (s32[1,1,4,16]{3,2,1,0:T(4,128)S(1)}, s32[1,1,4,16]{3,2,1,0:T(4,128)}, u32[]{:S(2)}) copy-start(s32[1,1,4,16]{3,2,1,0:T(4,128)} %param.24) | copy-start | bytes 772
  483.9 116.8 %all-to-all-start.1 = ((f32[8192,32,4]{0,2,1:T(4,128)}), f32[8192,32,4]{0,2,1:T(4,128)}, u32[]{:S(2)}, u32[]{:S(2)}) async-start(f32[8192,32,4]{0,2,1:T(4,128)} %copy.183), calls=%async_computation.1 | async-start | bytes 8388608 | tf_op jit(solution)/shard_map/all_to_all | solution.py:219
  487.5 121.7 %copy-start.54 = (f32[128]{0:T(128)S(1)}, f32[128]{0:T(128)}, u32[]{:S(2)}) copy-start(f32[128]{0:T(128)} %param.30) | copy-start | bytes 1540
  487.5 23.2 %collective-permute-start.1 = (f32[1,1,3,512]{3,1,2,0:T(1,128)S(1)}, f32[1,1,3,512]{3,1,2,0:T(1,128)S(1)}, u32[]{:S(2)}, u32[]{:S(2)}) collective-permute-start(f32[1,1,3,512]{3,1,2,0:T(1,128)S(1)} %copy-done.11), channel_id=1, source_target_pairs={{8,0},{16,8},{24,16},{0,24},{9,1},{17,9},{25,17},{1,25},{10,2},{18... | collective-permute-start | bytes 18440 | tf_op jit(solution)/shard_map/ppermute | solution.py:22
  488.8 21.9 %collective-permute-start = (f32[1,1,3,512]{3,1,2,0:T(1,128)S(1)}, f32[1,1,3,512]{3,1,2,0:T(1,128)S(1)}, u32[]{:S(2)}, u32[]{:S(2)}) collective-permute-start(f32[1,1,3,512]{3,1,2,0:T(1,128)S(1)} %copy-done.11), channel_id=1, source_target_pairs={{0,8},{8,16},{16,24},{24,0},{1,9},{9,17},{17,25},{25,1},{2,10},{10... | collective-permute-start | bytes 18440 | tf_op jit(solution)/shard_map/ppermute | solution.py:19
  489.2 73.5 %collective-permute-start.5 = (f32[1,1,512,128]{3,2,1,0:T(8,128)S(1)}, f32[1,1,512,128]{3,2,1,0:T(8,128)S(1)}, u32[]{:S(2)}, u32[]{:S(2)}) collective-permute-start(f32[1,1,512,128]{3,2,1,0:T(8,128)S(1)} %convolution_bitcast_fusion), channel_id=1, source_target_pairs={{8,0},{16,8},{24,16},{0,24},{9,1},{17,9},{25,17},{1,25},{10,2},{18... | collective-permute-start | bytes 786440 | tf_op jit(solution)/shard_map/ppermute | solution.py:22
  491.0 71.7 %collective-permute-start.4 = (f32[1,1,512,128]{3,2,1,0:T(8,128)S(1)}, f32[1,1,512,128]{3,2,1,0:T(8,128)S(1)}, u32[]{:S(2)}, u32[]{:S(2)}) collective-permute-start(f32[1,1,512,128]{3,2,1,0:T(8,128)S(1)} %convolution_bitcast_fusion), channel_id=1, source_target_pairs={{0,8},{8,16},{16,24},{24,0},{1,9},{9,17},{17,25},{25,1},{2,10},{10... | collective-permute-start | bytes 786440 | tf_op jit(solution)/shard_map/ppermute | solution.py:19
  510.7 48.1 %collective-permute-start.3 = (f32[3,1,3,512]{3,1,2,0:T(1,128)S(1)}, f32[3,1,3,512]{3,1,2,0:T(1,128)S(1)}, u32[]{:S(2)}, u32[]{:S(2)}) collective-permute-start(f32[3,1,3,512]{3,1,2,0:T(1,128)S(1)} %constant_dynamic-update-slice_fusion), channel_id=1, source_target_pairs={{1,0},{2,1},{3,2},{4,3},{5,4},{6,5},{7,6},{0,7},{9,8},{10,9},{11,1... | collective-permute-start | bytes 55304 | tf_op jit(solution)/shard_map/ppermute | solution.py:22
  524.3 38.1 %collective-permute-start.2 = (f32[3,1,3,512]{3,1,2,0:T(1,128)S(1)}, f32[3,1,3,512]{3,1,2,0:T(1,128)S(1)}, u32[]{:S(2)}, u32[]{:S(2)}) collective-permute-start(f32[3,1,3,512]{3,1,2,0:T(1,128)S(1)} %constant_dynamic-update-slice_fusion), channel_id=1, source_target_pairs={{0,1},{1,2},{2,3},{3,4},{4,5},{5,6},{6,7},{7,0},{8,9},{9,10},{10,1... | collective-permute-start | bytes 55304 | tf_op jit(solution)/shard_map/ppermute | solution.py:19
  562.7 55.4 %copy-start.4 = (f32[1,1,512,128]{3,2,1,0:T(8,128)}, f32[1,1,512,128]{3,2,1,0:T(8,128)S(1)}, u32[]{:S(2)}) copy-start(f32[1,1,512,128]{3,2,1,0:T(8,128)S(1)} %collective-permute-done.5) | copy-start | bytes 786436
  562.7 55.3 %copy-start.5 = (f32[1,1,512,128]{3,2,1,0:T(8,128)}, f32[1,1,512,128]{3,2,1,0:T(8,128)S(1)}, u32[]{:S(2)}) copy-start(f32[1,1,512,128]{3,2,1,0:T(8,128)S(1)} %collective-permute-done.4) | copy-start | bytes 786436
  562.8 65.3 %collective-permute-start.7 = (f32[3,1,512,128]{3,2,1,0:T(8,128)S(1)}, f32[3,1,512,128]{3,2,1,0:T(8,128)S(1)}, u32[]{:S(2)}, u32[]{:S(2)}) collective-permute-start(f32[3,1,512,128]{3,2,1,0:T(8,128)S(1)} %pad_maximum_fusion.2), channel_id=1, source_target_pairs={{1,0},{2,1},{3,2},{4,3},{5,4},{6,5},{7,6},{0,7},{9,8},{10,9},{11,1... | collective-permute-start | bytes 2359304 | tf_op jit(solution)/shard_map/ppermute | solution.py:22
  564.5 64.5 %collective-permute-start.6 = (f32[3,1,512,128]{3,2,1,0:T(8,128)S(1)}, f32[3,1,512,128]{3,2,1,0:T(8,128)}, u32[]{:S(2)}, u32[]{:S(2)}) collective-permute-start(f32[3,1,512,128]{3,2,1,0:T(8,128)S(1)} %pad_maximum_fusion.2), channel_id=1, source_target_pairs={{0,1},{1,2},{2,3},{3,4},{4,5},{5,6},{6,7},{7,0},{8,9},{9,10},{10,1... | collective-permute-start | bytes 2359304 | tf_op jit(solution)/shard_map/ppermute | solution.py:19
  625.8 4.9 collective-permute-start.10
  631.6 196.5 %collective-permute-start.11 = (f32[17,64,128]{2,1,0:T(8,128)}, f32[17,64,128]{2,1,0:T(8,128)}, u32[]{:S(2)}, u32[]{:S(2)}) collective-permute-start(f32[17,64,128]{2,1,0:T(8,128)} %fusion.75), channel_id=1, source_target_pairs={{0,7},{1,0},{2,1},{3,2},{4,3},{5,4},{6,5},{7,6},{8,15},{9,8},{10,9... | collective-permute-start | bytes 1671176 | tf_op jit(solution)/shard_map/ppermute | solution.py:29
  (98 other events, 1105.7 us)
where the time goes:
time: 878 us; the launch traced here: 866 us
  matrix products  344 us (39%)
  waiting for transfers between devices  200 us (23%)
  local copies, waits for them, and re-layouts  147 us (17%)
  other arithmetic  142 us (16%)
  starting transfers between devices  29.7 us (3%)
    all_to_all x1, waiting for transfers between devices, on_device(): lax.all_to_all(slab.reshape(slab_cells, devices, local_channels), ('wide'...  93.4 us
    dot_general x16, matrix products, one_slot(): jnp.einsum('tbij,tjc->tbic', basis_vals, other_val, precision=exact)  87.6 us
    scatter-add x8, other arithmetic, on_device(): spread.at[cell_list[corner]].add(weights[corner][:, None] * charges)  59.8 us
    dot_general x4, matrix products, rotate(): cos_real = jnp.einsum(subscripts, real_part, table_cos, precision=exact)  53.1 us
    dot_general x4, matrix products, rotate(): sin_real = jnp.einsum(subscripts, real_part, table_sin, precision=exact)  52.7 us
    dot_general x4, matrix products, rotate(): cos_imag = jnp.einsum(subscripts, imag_part, table_cos, precision=exact)  46.4 us
    dot_general x4, matrix products, rotate(): sin_imag = jnp.einsum(subscripts, imag_part, table_sin, precision=exact)  45.3 us
    all_to_all x1, waiting for transfers between devices, on_device(): lax.all_to_all(outgoing.reshape(slab_cells, devices, local_channels), ('w...  35.8 us
  transfers between devices with their start and end apart: 14, of which 7 were waited for; matrix products, arithmetic and copies ran while one was open for 27% of the time, Pallas kernels for 0%

commit v1 on v0

v1 whole, which is shorter than its diff:
```python
import jax
import jax.numpy as jnp
from jax import lax
from jax.sharding import PartitionSpec as P

MESH = 64
TILE = 128


fine = lax.Precision.HIGH


def extended_2(block, sides, width):
    for axis, dim in sides:
        count = lax.axis_size(axis)
        forward = [(i, i + 1) for i in range(count - 1)]
        forward.append((count - 1, 0))
        backward = [(target, source) for source, target in forward]
        low = lax.ppermute(
            lax.slice_in_dim(block, block.shape[dim] - width, None, axis=dim), axis, forward
        )
        high = lax.ppermute(lax.slice_in_dim(block, 0, width, axis=dim), axis, backward)
        block = jnp.concatenate([low, block, high], axis=dim)
    return block


def passed_along(array, axis, by):
    count = lax.axis_size(axis)
    return lax.ppermute(array, axis, [(i, (i + by) % count) for i in range(count)])


def short_range(near_values, near_positions, tile_codes, radial_mix, wide_count, sixteen_count):
    atom_count = near_values.shape[2]
    feature_width = near_values.shape[3]
    tiles_per = atom_count // TILE
    basis_count = radial_mix.shape[0]
    empty_code = 9 * tiles_per
    cutoff = 0.8 / max(wide_count, sixteen_count)
    sharpness = 0.5 * (basis_count - 1) ** 2
    centres = jnp.arange(basis_count).astype(jnp.float32) / (basis_count - 1)
    offsets = jnp.arange(3).astype(jnp.float32) - 1.0
    global_x = (near_positions[:, :, 0, :] + offsets[:, None, None]) / wide_count
    global_y = (near_positions[:, :, 1, :] + offsets[None, :, None]) / sixteen_count
    global_z = near_positions[:, :, 2, :]
    placed = jnp.stack([global_x, global_y, global_z], axis=2)
    source_pos = (
        placed.reshape(9, 3, tiles_per, TILE).transpose(0, 2, 1, 3).reshape(empty_code, 3, TILE)
    )
    source_val = near_values.reshape(empty_code, TILE, feature_width)
    own_pos = source_pos[4 * tiles_per : 5 * tiles_per]
    own_codes = 4 * tiles_per + jnp.arange(tiles_per, dtype=jnp.int32)
    diagonal = jnp.eye(TILE, dtype=bool)

    def one_slot(slot_index, running):
        slot_codes = tile_codes[:, slot_index]
        is_live = slot_codes < empty_code
        chosen = jnp.minimum(slot_codes, empty_code - 1)
        other_pos = source_pos[chosen]
        other_val = source_val[chosen]
        offset_vec = other_pos[:, :, None, :] - own_pos[:, :, :, None]
        delta_z = offset_vec[:, 2] - jnp.floor(offset_vec[:, 2] + 0.5)
        radius = jnp.sqrt(offset_vec[:, 0] ** 2 + offset_vec[:, 1] ** 2 + delta_z**2) / cutoff
        envelope = jnp.where(radius < 1.0, 0.5 * (jnp.cos(jnp.pi * radius) + 1.0), 0.0)
        itself = (slot_codes == own_codes)[:, None, None] & diagonal[None]
        envelope = jnp.where(is_live[:, None, None] & ~itself, envelope, 0.0)
        basis_vals = (
            jnp.exp(-sharpness * (radius[:, :, None] - centres[None, None, :, None]) ** 2)
            * envelope[:, :, None]
        )
        mixed = other_val[:, None] * radial_mix[None, :, None, :]
        return running + jnp.einsum(
            "tik,tkc->tic",
            basis_vals.reshape(tiles_per, TILE, basis_count * TILE),
            mixed.reshape(tiles_per, basis_count * TILE, feature_width),
            precision=fine,
        )

    live_slots = jnp.max(jnp.sum((tile_codes < empty_code).astype(jnp.int32), axis=1))
    running = lax.fori_loop(
        0, live_slots, one_slot, jnp.zeros((tiles_per, TILE, feature_width), jnp.float32)
    )
    return running.reshape(atom_count, feature_width)


def hat(coords, count):
    return jnp.maximum(
        1.0 - jnp.abs(coords[..., None] - jnp.arange(count).astype(jnp.float32)), 0.0
    )


def plane_weights(pos, step_x, step_y, slab_x, slab_y, count_x, count_y):
    atoms = pos.shape[1]
    per_plane = atoms // MESH
    plane = (jnp.arange(atoms, dtype=jnp.int32) // per_plane).astype(jnp.float32)
    upper = pos[2] * MESH - plane
    flat = (
        hat((pos[0] + step_x) * slab_x, count_x)[:, :, None]
        * hat((pos[1] + step_y) * slab_y, count_y)[:, None, :]
    ).reshape(MESH, per_plane, count_x * count_y)
    upper = upper.reshape(MESH, per_plane, 1)
    return jnp.concatenate([flat * (1.0 - upper), jnp.roll(flat * upper, 1, axis=0)], axis=1)


def filter_kernel(screening, smearing):
    sample_index = jnp.arange(MESH, dtype=jnp.int32)
    signed = jnp.where(sample_index < MESH // 2, sample_index, sample_index - MESH).astype(
        jnp.float32
    )
    wavenumber = 2.0 * jnp.pi * signed
    squares = (
        wavenumber[:, None, None] ** 2
        + wavenumber[None, :, None] ** 2
        + wavenumber[None, None, :] ** 2
    )
    kappa_sq = screening[:, None, None, None] ** 2
    return (
        kappa_sq
        * jnp.exp(-0.5 * squares[None] * smearing[:, None, None, None] ** 2)
        / (squares[None] + kappa_sq)
    )


def smooth_field(field_grid, screening, smearing):
    sample_index = jnp.arange(MESH, dtype=jnp.int32)
    phase_index = sample_index[:, None] * sample_index[None, :] % MESH
    angle_grid = phase_index.astype(jnp.float32) * (2.0 * jnp.pi / MESH)
    table = (jnp.cos(angle_grid) + jnp.sin(angle_grid)) * (MESH**-0.5)
    grid = jnp.einsum("cuvw,wk->cuvk", field_grid, table, precision=fine)
    grid = jnp.einsum("cuvw,vk->cukw", grid, table, precision=fine)
    grid = jnp.einsum("cuvw,uk->ckvw", grid, table, precision=fine)
    grid = grid * filter_kernel(screening, smearing)
    grid = jnp.einsum("cuvw,uk->ckvw", grid, table, precision=fine)
    grid = jnp.einsum("cuvw,vk->cukw", grid, table, precision=fine)
    return jnp.einsum("cuvw,wk->cuvk", grid, table, precision=fine)


def on_device(
    features,
    positions,
    tile_lists,
    value_proj,
    radial_mix,
    charge_proj,
    screening,
    smearing,
    mesh_gain,
    mesh_up,
    mesh_down,
    long_proj,
    atom_gain,
    atom_up,
    atom_down,
):
    wide_count = lax.axis_size("wide")
    sixteen_count = lax.axis_size("sixteen")
    devices = wide_count * sixteen_count
    channels = charge_proj.shape[1]
    local_channels = screening.shape[0]
    slab_x = MESH // wide_count
    slab_y = MESH // sixteen_count
    slab_cells = slab_x * slab_y * MESH
    near_features, near_positions = (
        extended_2(features, (("wide", 0), ("sixteen", 1)), 1),
        extended_2(positions, (("wide", 0), ("sixteen", 1)), 1),
    )
    own_features = features[0, 0]
    own_pos = positions[0, 0]
    atoms = own_features.shape[0]
    per_plane = atoms // MESH
    weights = []
    sources = []
    for step_x, step_y in ((0, 0), (-1, 0), (0, -1), (-1, -1)):
        weights.append(
            plane_weights(
                near_positions[1 + step_x, 1 + step_y],
                step_x, step_y, slab_x, slab_y, slab_x, slab_y,
            )
        )
        charges = jnp.dot(
            near_features[1 + step_x, 1 + step_y], charge_proj, precision=fine
        ).reshape(MESH, per_plane, channels)
        sources.append(jnp.concatenate([charges, jnp.roll(charges, 1, axis=0)], axis=1))
    slab = jnp.einsum(
        "zac,zan->zcn",
        jnp.concatenate(sources, axis=1),
        jnp.concatenate(weights, axis=1),
        precision=fine,
    ).transpose(1, 0, 2)
    grouped = lax.all_to_all(
        slab.reshape(devices, local_channels, MESH, slab_x * slab_y),
        ("wide", "sixteen"),
        split_axis=0,
        concat_axis=0,
        tiled=True,
    )
    values = jnp.einsum("xyaf,fg->xyag", near_features, value_proj, precision=fine)
    messages = short_range(
        values, near_positions, tile_lists[0, 0], radial_mix, wide_count, sixteen_count
    )
    grouped = grouped.reshape(wide_count, sixteen_count, local_channels, MESH, slab_x, slab_y)
    field_grid = grouped.transpose(2, 3, 0, 4, 1, 5).reshape(local_channels, MESH, MESH, MESH)
    potential = smooth_field(field_grid, screening, smearing)
    outgoing = potential.reshape(
        local_channels, MESH, wide_count, slab_x, sixteen_count, slab_y
    ).transpose(2, 4, 0, 1, 3, 5)
    by_cells = lax.all_to_all(
        outgoing.reshape(devices, local_channels, MESH, slab_x * slab_y),
        ("wide", "sixteen"),
        split_axis=0,
        concat_axis=0,
        tiled=True,
    ).reshape(channels, slab_cells)
    inverse_rms = lax.rsqrt(jnp.mean(by_cells**2, axis=0, keepdims=True) + 1e-06)
    normed = by_cells * inverse_rms * mesh_gain[:, None]
    hidden = jax.nn.silu(jnp.einsum("cn,ch->nh", normed, mesh_up, precision=fine))
    mesh_out = jnp.dot(hidden, mesh_down, precision=fine).reshape(MESH, slab_x, slab_y, channels)
    face_x = passed_along(mesh_out[:, 0], "wide", -1)
    face_y = passed_along(
        jnp.concatenate([mesh_out[:, :, 0], face_x[:, :1]], axis=1), "sixteen", -1
    )
    corners = plane_weights(
        own_pos, 0, 0, slab_x, slab_y, slab_x + 1, slab_y + 1
    ).reshape(MESH, 2 * per_plane, slab_x + 1, slab_y + 1)
    gathered = jnp.einsum(
        "zan,znc->zac",
        corners[:, :, :slab_x, :slab_y].reshape(MESH, 2 * per_plane, slab_x * slab_y),
        mesh_out.reshape(MESH, slab_x * slab_y, channels),
        precision=fine,
    )
    gathered += jnp.einsum("zan,znc->zac", corners[:, :, slab_x, :slab_y], face_x, precision=fine)
    gathered += jnp.einsum("zan,znc->zac", corners[:, :, :, slab_y], face_y, precision=fine)
    at_atoms = gathered[:, :per_plane] + jnp.roll(gathered[:, per_plane:], -1, axis=0)
    long_terms = jnp.dot(at_atoms.reshape(atoms, channels), long_proj, precision=fine)
    summed = own_features + messages + long_terms
    inverse_rms = lax.rsqrt(jnp.mean(summed**2, axis=-1, keepdims=True) + 1e-06)
    normed = summed * inverse_rms * atom_gain
    hidden = jax.nn.silu(jnp.dot(normed, atom_up, precision=fine))
    updated = summed + jnp.dot(hidden, atom_down, precision=fine)
    return updated[None, None]


def solution(mesh):
    in_specs = (
        P("wide", "sixteen", None, None),
        P("wide", "sixteen", None, None),
        P("wide", "sixteen", None, None),
        P(),
        P(),
        P(),
        P(("wide", "sixteen")),
        P(("wide", "sixteen")),
        P(),
        P(),
        P(),
        P(),
        P(),
        P(),
        P(),
    )
    out_specs = P("wide", "sixteen", None, None)
    return jax.shard_map(
        on_device, mesh=mesh, in_specs=in_specs, out_specs=out_specs, check_vma=False
    )
```

time: 878 us -> 837 us (0.953)
  local copies, waits for them, and re-layouts: 147 us -> 358 us
  matrix products: 344 us -> 172 us
  other arithmetic: 142 us -> 61.8 us
  loops' own time: 1.79 us -> 13 us
  starting transfers between devices: 29.7 us -> 20.1 us
    dot_general x43 -> x36, matrix products: 344 us -> 172 us  [the longest x16 83.1 us: one_slot(): jnp.einsum('tik,tkc->tic', basis_vals.reshape(tiles_per, TILE, basis_coun...]
    mul x0 -> x61, local copies, waits for them, and re-layouts: none -> 138 us  [the longest x32 117 us: one_slot(): jnp.exp(-sharpness * (radius[:, :, None] - centres[None, None, :, None])...]
    sub x0 -> x49, local copies, waits for them, and re-layouts: none -> 116 us  [the longest x48 116 us: one_slot(): radius[:, :, None] - centres[None, None, :, None]]
    scatter-add x10 -> x0, other arithmetic: 60.7 us -> none  [the longest x8 59.8 us: on_device(): spread.at[cell_list[corner]].add(weights[corner][:, None] * charges)]
    all_to_all x2, waiting for transfers between devices: 129 us -> 98.8 us  [the longest x1 93.9 us: on_device(): lax.all_to_all(slab.reshape(devices, local_channels, MESH, slab_x * slab_...]
    ppermute x4, waiting for transfers between devices: 34.3 us -> 62.7 us  [extended_2(): lax.ppermute(lax.slice_in_dim(block, 0, width, axis=dim), axis, backward)]
    sub x17 -> x4, other arithmetic: 28.5 us -> 0.13 us  [plane_weights(): upper = pos[2] * MESH - plane]
    gather x8 -> x0, local copies, waits for them, and re-layouts: 27.7 us -> none  [on_device(): at_atoms = at_atoms + weights[corner][:, None] * extended[cell_list[corner]]]
  transfers between devices with their start and end apart: 14 -> 12, of which waited for: 7 -> 7; matrix products, arithmetic and copies ran while one was open for 27% -> 53% of each run, Pallas kernels for 0% -> 0%
where the time goes in v1:
time: 837 us; the launch traced here: 821 us
  local copies, waits for them, and re-layouts  358 us (43%)
  waiting for transfers between devices  194 us (23%)
  matrix products  172 us (21%)
  other arithmetic  61.8 us (7%)
  starting transfers between devices  20.1 us (2%)
  loops' own time  13 us (2%)
    mul x32, local copies, waits for them, and re-layouts, one_slot(): jnp.exp(-sharpness * (radius[:, :, None] - centres[None, None, :, None])...  117 us
    sub x48, local copies, waits for them, and re-layouts, one_slot(): radius[:, :, None] - centres[None, None, :, None]  116 us
    all_to_all x1, waiting for transfers between devices, on_device(): lax.all_to_all(slab.reshape(devices, local_channels, MESH, slab_x * slab_...  93.9 us
    dot_general x16, matrix products, one_slot(): jnp.einsum('tik,tkc->tic', basis_vals.reshape(tiles_per, TILE, basis_coun...  83.1 us
    ppermute x4, waiting for transfers between devices, extended_2(): lax.ppermute(lax.slice_in_dim(block, 0, width, axis=dim), axis, backward)  62.7 us
    while x96, local copies, waits for them, and re-layouts  27.6 us
    ppermute x4, waiting for transfers between devices, extended_2(): lax.ppermute(lax.slice_in_dim(block, block.shape[dim] - width, None, axis...  24.2 us
    mul x5, local copies, waits for them, and re-layouts, plane_weights(): hat((pos[0] + step_x) * slab_x, count_x)[:, :, None]  19.8 us
  transfers between devices with their start and end apart: 12, of which 7 were waited for; matrix products, arithmetic and copies ran while one was open for 53% of the time, Pallas kernels for 0%

profile of v1, /device:TPU:0, one launch (start us, length us, event | category | flops | bytes accessed | tf_op | source)
XLA Modules:
  0.0 820.8 jit_solution(7406028498291918915)
XLA Ops:
  56.7 19.5 %collective-permute-done.6 = f32[3,1,512,128]{3,2,1,0:T(8,128)S(1)} collective-permute-done((f32[3,1,512,128]{3,2,1,0:T(8,128)}, f32[3,1,512,128]{3,2,1,0:T(8,128)S(1)}, u32[]{:S(2)}, u32[]{:S(2)}) %collective-permute-start.6) | collective-permute-done | bytes 786464 | tf_op jit(solution)/shard_map/ppermute | solution.py:19
  94.8 93.9 %all-to-all-done = f32[32,4,64,128]{3,2,1,0:T(8,128)} async-done(((f32[32,4,64,128]{3,2,1,0:T(8,128)}), f32[32,4,64,128]{3,2,1,0:T(8,128)}, u32[]{:S(2)}, u32[]{:S(2)}) %all-to-all-start) | async-done | bytes 4194336 | tf_op jit(solution)/shard_map/all_to_all | solution.py:189
  188.8 7.0 copy.200
  195.7 7.8 copy.201
  203.6 8.8 %copy.202 = f32[4,64,64,64]{3,2,1,0:T(8,128)} copy(f32[4,64,64,64]{1,3,2,0:T(8,128)} %bitcast.222) | data formatting | bytes 8388608 | tf_op jit(solution)/shard_map/reshape | solution.py:201
  212.3 7.7 fusion.97
  224.4 9.0 %fusion.28 = f32[64,4,64,64]{3,0,2,1:T(8,128)S(1)} fusion(f32[4,64,64,64]{3,2,1,0:T(8,128)S(1)} %convolution_bitcast_fusion), kind=kOutput, calls=%fused_computation.41 | convolution fusion | flops 402718720 | bytes 8388608 | tf_op jit(solution)/shard_map/cuvw,uk->ckvw/dot_general | solution.py:130
  233.4 8.4 %fusion.50 = f32[4,64,64,64]{3,1,2,0:T(8,128)} fusion(f32[64,4,64,64]{3,0,2,1:T(8,128)S(1)} %fusion.28, f32[64,64,64]{2,0,1:T(8,128)S(1)} %copy-done.6, f32[4]{0:T(128)S(1)} %integer_pow.96, f32[64,64,64]{2,0,1:T(8,128)S(1)} %get-tuple-element.259, f32[4]{0:T(128)S(1)} %integer_pow.94), kind=kOutput, calls=%fused_computation.65 | convolution fusion | flops 407961600 | bytes 10485792 | tf_op jit(solution)/shard_map/cuvw,uk->ckvw/dot_general | solution.py:132
  241.7 12.8 %fusion.51 = f32[4,64,64,64]{3,2,1,0:T(8,128)S(1)} fusion(f32[4,64,64,64]{3,1,2,0:T(8,128)} %fusion.50), kind=kOutput, calls=%fused_computation.66 | convolution fusion | flops 402718720 | bytes 8388608 | tf_op jit(solution)/shard_map/cuvw,vk->cukw/dot_general | solution.py:133
  254.5 14.7 %fusion.24 = f32[4,64,64,64]{1,3,2,0:T(8,128)S(1)} fusion(f32[4,64,64,64]{3,2,1,0:T(8,128)S(1)} %fusion.51), kind=kOutput, calls=%fused_computation.37 | convolution fusion | flops 402718720 | bytes 8388608 | tf_op jit(solution)/shard_map/cuvw,wk->cuvk/dot_general | solution.py:134
  273.9 6.8 copy.211
  309.6 46.4 %collective-permute-done.3 = f32[3,1,3,512]{3,1,2,0:T(1,128)S(1)} collective-permute-done((f32[3,1,3,512]{3,1,2,0:T(1,128)S(1)}, f32[3,1,3,512]{3,1,2,0:T(1,128)S(1)}, u32[]{:S(2)}, u32[]{:S(2)}) %collective-permute-start.3) | collective-permute-done | bytes 18464 | tf_op jit(solution)/shard_map/ppermute | solution.py:22
  356.3 16.3 %collective-permute-done.7 = f32[3,1,512,128]{3,2,1,0:T(8,128)} collective-permute-done((f32[3,1,512,128]{3,2,1,0:T(8,128)}, f32[3,1,512,128]{3,2,1,0:T(8,128)}, u32[]{:S(2)}, u32[]{:S(2)}) %collective-permute-start.7) | collective-permute-done | bytes 786464 | tf_op jit(solution)/shard_map/ppermute | solution.py:22
  382.7 7.8 fusion.42
  397.4 402.2 %while.13 = (s32[]{:T(128)}, f32[4,128,128]{2,1,0:T(8,128)S(1)}, s32[]{:T(128)}, s32[4,16]{0,1:T(8,128)S(1)}, f32[36,3,128]{2,1,0:T(4,128)S(1)}, /*index=5*/f32[...) while((s32[]{:T(128)}, f32[4,128,128]{2,1,0:T(8,128)S(1)}, ...), condition=%wide.region_3.4_spmd.clone, body=%wide.region_2.3_spmd.clone.sunk | while | flops 812008512 | bytes 65290712 | solution.py:79
  417.2 5.2 fusion.186
  467.4 5.2 fusion.186
  492.5 5.2 fusion.186
  517.6 5.2 fusion.186
  567.7 5.2 fusion.186
  643.0 5.2 fusion.186
  718.2 5.2 fusion.186
  793.5 5.2 fusion.186
  808.8 8.5 %collective-permute-done.9 = f32[64,17,128]{2,0,1:T(8,128)S(1)} collective-permute-done((f32[64,17,128]{2,0,1:T(8,128)S(1)}, f32[64,17,128]{2,0,1:T(8,128)S(1)}, u32[]{:S(2)}, u32[]{:S(2)}) %collective-permute-start.9) | collective-permute-done | bytes 557088 | tf_op jit(solution)/shard_map/ppermute | solution.py:29
  (592 shorter events, 489.5 us)
Async XLA Ops:
  0.0 382.7 %copy-start = (f32[128,256]{1,0:T(8,128)S(1)}, f32[128,256]{1,0:T(8,128)}, u32[]{:S(2)}) copy-start(f32[128,256]{1,0:T(8,128)} %param.26) | copy-start | bytes 393220
  0.0 8.4 %collective-permute-start = (f32[1,1,3,512]{3,1,2,0:T(1,128)}, f32[1,1,3,512]{3,1,2,0:T(1,128)S(1)}, u32[]{:S(2)}, u32[]{:S(2)}) collective-permute-start(f32[1,1,3,512]{3,1,2,0:T(1,128)} %param.18), channel_id=1, source_target_pairs={{0,8},{8,16},{16,24},{24,0},{1,9},{9,17},{17,25},{25,1},{2,10},{10... | collective-permute-start | bytes 18440 | tf_op jit(solution)/shard_map/ppermute | solution.py:19
  0.5 8.6 %collective-permute-start.1 = (f32[1,1,3,512]{3,1,2,0:T(1,128)}, f32[1,1,3,512]{3,1,2,0:T(1,128)S(1)}, u32[]{:S(2)}, u32[]{:S(2)}) collective-permute-start(f32[1,1,3,512]{3,1,2,0:T(1,128)} %param.18), channel_id=1, source_target_pairs={{8,0},{16,8},{24,16},{0,24},{9,1},{17,9},{25,17},{1,25},{10,2},{18... | collective-permute-start | bytes 18440 | tf_op jit(solution)/shard_map/ppermute | solution.py:22
  2.5 48.8 %collective-permute-start.4 = (f32[1,1,512,128]{3,2,1,0:T(8,128)}, f32[1,1,512,128]{3,2,1,0:T(8,128)S(1)}, u32[]{:S(2)}, u32[]{:S(2)}) collective-permute-start(f32[1,1,512,128]{3,2,1,0:T(8,128)} %param.17), channel_id=1, source_target_pairs={{0,8},{8,16},{16,24},{24,0},{1,9},{9,17},{17,25},{25,1},{2,10},{10... | collective-permute-start | bytes 786440 | tf_op jit(solution)/shard_map/ppermute | solution.py:19
  3.1 49.7 %collective-permute-start.5 = (f32[1,1,512,128]{3,2,1,0:T(8,128)}, f32[1,1,512,128]{3,2,1,0:T(8,128)}, u32[]{:S(2)}, u32[]{:S(2)}) collective-permute-start(f32[1,1,512,128]{3,2,1,0:T(8,128)} %param.17), channel_id=1, source_target_pairs={{8,0},{16,8},{24,16},{0,24},{9,1},{17,9},{25,17},{1,25},{10,2},{18... | collective-permute-start | bytes 786440 | tf_op jit(solution)/shard_map/ppermute | solution.py:22
  5.5 19.6 %copy-start.20 = (f32[1,1,1,512]{3,1,2,0:T(1,128)}, f32[1,1,1,512]{3,1,2,0:T(1,128)S(1)}, u32[]{:S(2)}) copy-start(f32[1,1,1,512]{3,1,2,0:T(1,128)S(1)} %get-tuple-element.279) | copy-start | bytes 6148
  9.1 16.0 %copy-start.18 = (f32[3,1,3,512]{3,1,2,0:T(1,128)}, f32[3,1,3,512]{3,1,2,0:T(1,128)S(1)}, u32[]{:S(2)}) copy-start(f32[3,1,3,512]{3,1,2,0:T(1,128)S(1)} %constant_dynamic-update-slice_fusion) | copy-start | bytes 55300
  9.1 7.1 collective-permute-start.2
  54.4 21.8 %collective-permute-start.6 = (f32[3,1,512,128]{3,2,1,0:T(8,128)}, f32[3,1,512,128]{3,2,1,0:T(8,128)S(1)}, u32[]{:S(2)}, u32[]{:S(2)}) collective-permute-start(f32[3,1,512,128]{3,2,1,0:T(8,128)} %constant_dynamic-update-slice_fusion.3), channel_id=1, source_target_pairs={{0,1},{1,2},{2,3},{3,4},{4,5},{5,6},{6,7},{7,0},{8,9},{9,10},{10,1... | collective-permute-start | bytes 2359304 | tf_op jit(solution)/shard_map/ppermute | solution.py:19
  89.3 99.5 %all-to-all-start = ((f32[32,4,64,128]{3,2,1,0:T(8,128)}), f32[32,4,64,128]{3,2,1,0:T(8,128)}, u32[]{:S(2)}, u32[]{:S(2)}) async-start(f32[32,4,64,128]{3,2,1,0:T(8,128)} %copy.199), calls=%async_computation | async-start | bytes 8388608 | tf_op jit(solution)/shard_map/all_to_all | solution.py:189
  280.7 99.5 %all-to-all-start.1 = ((f32[32,4,64,128]{3,2,1,0:T(8,128)}), f32[32,4,64,128]{3,2,1,0:T(8,128)}, u32[]{:S(2)}, u32[]{:S(2)}) async-start(f32[32,4,64,128]{3,2,1,0:T(8,128)} %copy.211), calls=%async_computation.1 | async-start | bytes 8388608 | tf_op jit(solution)/shard_map/all_to_all | solution.py:206
  300.3 55.7 %copy-start.17 = (f32[3,1,3,512]{3,1,2,0:T(1,128)S(1)}, f32[3,1,3,512]{3,1,2,0:T(1,128)}, u32[]{:S(2)}) copy-start(f32[3,1,3,512]{3,1,2,0:T(1,128)} %copy-done.16) | copy-start | bytes 55300
  300.4 55.6 %collective-permute-start.3 = (f32[3,1,3,512]{3,1,2,0:T(1,128)S(1)}, f32[3,1,3,512]{3,1,2,0:T(1,128)S(1)}, u32[]{:S(2)}, u32[]{:S(2)}) collective-permute-start(f32[3,1,3,512]{3,1,2,0:T(1,128)S(1)} %copy-done.19), channel_id=1, source_target_pairs={{1,0},{2,1},{3,2},{4,3},{5,4},{6,5},{7,6},{0,7},{9,8},{10,9},{11,1... | collective-permute-start | bytes 55304 | tf_op jit(solution)/shard_map/ppermute | solution.py:22
  304.9 67.6 %collective-permute-start.7 = (f32[3,1,512,128]{3,2,1,0:T(8,128)}, f32[3,1,512,128]{3,2,1,0:T(8,128)}, u32[]{:S(2)}, u32[]{:S(2)}) collective-permute-start(f32[3,1,512,128]{3,2,1,0:T(8,128)} %constant_dynamic-update-slice_fusion.3), channel_id=1, source_target_pairs={{1,0},{2,1},{3,2},{4,3},{5,4},{6,5},{7,6},{0,7},{9,8},{10,9},{11,1... | collective-permute-start | bytes 2359304 | tf_op jit(solution)/shard_map/ppermute | solution.py:22
  356.3 26.4 %copy-start.28 = (f32[128]{0:T(128)S(1)}, f32[128]{0:T(128)}, u32[]{:S(2)}) copy-start(f32[128]{0:T(128)} %param.25) | copy-start | bytes 1540
  396.1 406.3 %collective-permute-start.8 = (f32[64,8,128]{2,1,0:T(8,128)}, f32[64,8,128]{2,1,0:T(8,128)}, u32[]{:S(2)}, u32[]{:S(2)}) collective-permute-start(f32[64,8,128]{2,1,0:T(8,128)} %slice_bitcast_fusion.1), channel_id=1, source_target_pairs={{0,24},{8,0},{16,8},{24,16},{1,25},{9,1},{17,9},{25,17},{2,26},{10... | collective-permute-start | bytes 786440 | tf_op jit(solution)/shard_map/ppermute | solution.py:29
  802.4 14.9 %copy-start.7 = (f32[64,16,17,1]{2,1,0,3:T(8,128)S(1)}, f32[64,16,17,1]{2,1,0,3:T(8,128)}, u32[]{:S(2)}) copy-start(f32[64,16,17,1]{2,1,0,3:T(8,128)} %copy.244) | copy-start | bytes 208900
  803.5 13.8 %collective-permute-start.9 = (f32[64,17,128]{2,0,1:T(8,128)S(1)}, f32[64,17,128]{2,0,1:T(8,128)S(1)}, u32[]{:S(2)}, u32[]{:S(2)}) collective-permute-start(f32[64,17,128]{2,0,1:T(8,128)S(1)} %pad_maximum_fusion.1), channel_id=1, source_target_pairs={{0,7},{1,0},{2,1},{3,2},{4,3},{5,4},{6,5},{7,6},{8,15},{9,8},{10,9... | collective-permute-start | bytes 1671176 | tf_op jit(solution)/shard_map/ppermute | solution.py:29
  803.6 14.5 %copy-start.9 = (f32[1,1,512,128]{2,3,1,0:T(8,128)S(1)}, f32[1,1,512,128]{2,3,1,0:T(8,128)}, u32[]{:S(2)}) copy-start(f32[1,1,512,128]{2,3,1,0:T(8,128)} %copy.181) | copy-start | bytes 786436
  803.6 14.5 %copy-start.15 = (f32[128,128]{1,0:T(8,128)S(1)}, f32[128,128]{1,0:T(8,128)}, u32[]{:S(2)}) copy-start(f32[128,128]{1,0:T(8,128)} %param.28) | copy-start | bytes 196612
  807.1 11.3 %copy-start.14 = (f32[128,256]{1,0:T(8,128)S(1)}, f32[128,256]{1,0:T(8,128)}, u32[]{:S(2)}) copy-start(f32[128,256]{1,0:T(8,128)} %param.30) | copy-start | bytes 393220
  807.1 11.3 %copy-start.29 = (f32[128]{0:T(128)S(1)}, f32[128]{0:T(128)}, u32[]{:S(2)}) copy-start(f32[128]{0:T(128)} %param.29) | copy-start | bytes 1540
  807.2 11.8 %copy-start.31 = (f32[256,128]{1,0:T(8,128)S(1)}, f32[256,128]{1,0:T(8,128)}, u32[]{:S(2)}) copy-start(f32[256,128]{1,0:T(8,128)} %param.31) | copy-start | bytes 393220
  807.2 13.2 %copy-start.1 = (f32[128,256]{1,0:T(8,128)S(1)}, f32[128,256]{1,0:T(8,128)}, u32[]{:S(2)}) copy-start(f32[128,256]{1,0:T(8,128)} %param.26) | copy-start | bytes 393220
  (67 other events, 224.6 us)
